TPU v7x, 32 devices: a whole 2x2x4 slice. The times are simulated.
32 devices in a mesh: slab: 8 (over z, y), mem: 4 (over x, core).
Axes of the slice: x: 2, y: 2, z: 4, core: 2. Of those that a mesh axis runs over, the one named last changes fastest.
Arguments:
- starting_states_set: float32 [128, 64, 1024], P('mem', 'slab'), may hold values from -6 to 6
- land_mask: int32 [64, 1024], P('slab'), may hold values 0 or 1
- cell_class: int32 [64, 1024], P('slab'), may hold values from 0 to 7
- kappa_table: float32 [8], replicated, may hold values from 0.08 to 0.2
- flow_table: float32 [2, 8], replicated, may hold values from -0.3 to 0.3
- obs_index: int32 [1024], P('slab'), may hold values from 0 to 8191
- obs_values: float32 [1024], P('slab'), may hold values from -24 to 24
- obs_var: float32 [1024], P('slab'), may hold values from 0.1 to 1
Outputs:
- analysis: float32 [128, 64, 1024], P('mem', 'slab')
All inputs are finite; a program needn't handle non-finite values. No bound on the sum of `land_mask` on one device may be relied on, other than what follows from the above.
Results may differ from a plain program's by a relative error of at most 0.00016.
Values sent between devices are 32-bit elements; how exact they have to be, the bound alone decides.
A program may use at most 64 MiB of HBM per device.

v0:
```python
import jax
import jax.numpy as jnp
from jax import lax
from jax.sharding import PartitionSpec as P

STEPS = 8
ROOT_ITERATIONS = 8
NCLS = 8


def extended(block, sides, width):
    for axis, dim in sides:
        count = lax.axis_size(axis)
        forward = [(i, i + 1) for i in range(count - 1)]
        backward = [(target, source) for source, target in forward]
        low = lax.ppermute(
            lax.slice_in_dim(block, block.shape[dim] - width, None, axis=dim), axis, forward
        )
        high = lax.ppermute(lax.slice_in_dim(block, 0, width, axis=dim), axis, backward)
        block = jnp.concatenate([low, block, high], axis=dim)
    return block


def advance(center, north, south, diffusion, flow_east, flow_north, wet_cells):
    edge = jnp.zeros_like(center[..., :1])
    east = jnp.concatenate([center[..., 1:], edge], axis=-1)
    west = jnp.concatenate([edge, center[..., :-1]], axis=-1)
    spread = north + south + east + west - 4.0 * center
    return wet_cells * (
        center
        + diffusion * spread
        - 0.5 * flow_east * (east - west)
        - 0.5 * flow_north * (north - south)
    )


def coefficients(classes, mask_rows, kappa_table, flow_table):
    diffusion = jnp.zeros(classes.shape, jnp.float32)
    flow_east = jnp.zeros(classes.shape, jnp.float32)
    flow_north = jnp.zeros(classes.shape, jnp.float32)
    for label in range(NCLS):
        hit = classes == label
        diffusion = diffusion + jnp.where(hit, kappa_table[label], 0.0)
        flow_east = flow_east + jnp.where(hit, flow_table[0, label], 0.0)
        flow_north = flow_north + jnp.where(hit, flow_table[1, label], 0.0)
    return (diffusion, flow_east, flow_north, mask_rows.astype(jnp.float32))


def statistics(observed, values, variances, factor, ens_total):
    highest = lax.Precision.HIGHEST
    ybar = jnp.sum(observed, axis=0) / ens_total
    err = variances * factor
    anom = (observed - ybar) / jnp.sqrt(err * (ens_total - 1.0))
    dev = (values - ybar) / jnp.sqrt(err)
    return (jnp.dot(anom, anom.T, precision=highest), jnp.dot(anom, dev, precision=highest))


def local(
    starting_states_set,
    land_mask,
    cell_class,
    kappa_table,
    flow_table,
    obs_index,
    obs_values,
    obs_var,
):
    highest = lax.Precision.HIGHEST
    kd = starting_states_set.shape[0]
    rows = starting_states_set.shape[1]
    ens_total = kd * lax.axis_size("mem")
    current_profile = starting_states_set
    diffusion, flow_east, flow_north, wet_cells = coefficients(
        cell_class, land_mask, kappa_table, flow_table
    )
    for step in range(STEPS):
        padded = extended(current_profile, (("slab", 1),), 1)
        current_profile = advance(
            padded[:, 1:-1],
            padded[:, 2:],
            padded[:, :-2],
            diffusion,
            flow_east,
            flow_north,
            wet_cells,
        )
    raveled_vector = current_profile.reshape(kd, rows * current_profile.shape[2])
    observed = jnp.take(raveled_vector, obs_index, axis=1)
    slab_here = lax.axis_index("slab").astype(jnp.float32)
    factor = 1.0 + 2.0 * slab_here / float(lax.axis_size("slab") - 1)
    member_group = lax.axis_index("mem")
    columns = lax.all_to_all(observed, "mem", split_axis=1, concat_axis=0, tiled=True)
    count = columns.shape[1]
    values = lax.dynamic_slice_in_dim(obs_values, member_group * count, count)
    variances = lax.dynamic_slice_in_dim(obs_var, member_group * count, count)
    gram_part, proj_part = statistics(columns, values, variances, factor, ens_total)
    gram, proj = lax.psum((gram_part, proj_part), ("slab", "mem"))
    ident = jnp.eye(ens_total, dtype=jnp.float32)
    matrix = ident + gram
    scale = jnp.trace(matrix)
    upper = matrix / scale
    lower = ident
    for turn in range(ROOT_ITERATIONS):
        factor_q = 1.5 * ident - 0.5 * jnp.dot(lower, upper, precision=highest)
        upper = jnp.dot(upper, factor_q, precision=highest)
        lower = jnp.dot(factor_q, lower, precision=highest)
    transform_weights = lower / jnp.sqrt(scale)
    mean_w = jnp.dot(lower, jnp.dot(lower, proj, precision=highest), precision=highest) / (
        scale * jnp.sqrt(ens_total - 1.0)
    )
    total_w = transform_weights + mean_w[:, None]
    omega = 1.0 / ens_total + total_w - (jnp.sum(total_w, axis=0) / ens_total)[None, :]
    mixed = jnp.einsum(
        "ij,irc->jrc",
        omega,
        lax.all_to_all(current_profile, "mem", split_axis=2, concat_axis=0, tiled=True),
        precision=highest,
    )
    return lax.all_to_all(mixed, "mem", split_axis=0, concat_axis=2, tiled=True)


def solution(mesh):
    return jax.shard_map(
        local,
        mesh=mesh,
        in_specs=(
            P("mem", "slab", None),
            P("slab", None),
            P("slab", None),
            P(),
            P(),
            P("slab"),
            P("slab"),
            P("slab"),
        ),
        out_specs=P("mem", "slab", None),
        check_vma=False,
    )
```

profile of v0, /device:TPU:0, one launch (start us, length us, event | category | flops | bytes accessed | tf_op | source)
XLA Modules:
  0.0 308.6 jit_solution(16976725727790895447)
XLA Ops:
  6.5 1.9 copy.42
  9.2 1.3 collective-permute-start
  10.5 5.5 %collective-permute-start.1 = (f32[32,1,1024]{2,0,1:T(8,128)}, f32[32,1,1024]{2,0,1:T(8,128)S(1)}, u32[]{:S(2)}, u32[]{:S(2)}) collective-permute-start(f32[32,1,1024]{2,0,1:T(8,128)} %get-tuple-element.42), channel_id=1, source_target_pairs={{0,4},{4,8},{8,12},{12,16},{16,20},{20,24},{24,28},{1,5},{5,9},{9,... | collective-permute-start | bytes 393224 | tf_op jit(solution)/shard_map/ppermute | solution.py:16
  17.8 5.0 %select_add_fusion = (f32[8,1024]{1,0:T(8,128)S(1)}, pred[8,1024]{1,0:T(8,128)(4,1)S(1)}, pred[8,1024]{1,0:T(8,128)(4,1)S(1)}, pred[8,1024]{1,0:T(8,128)(4,1)S(1...) fusion(f32[]{:T(128)} %bitcast.7, f32[]{:T(128)} %bitcast.6, ...), kind=kLoop, calls=%fused_computation.61 | loop fusion | flops 188416 | bytes 131104 | tf_op jit(solution)/shard_map/add | solution.py:43
  22.8 5.0 %add_multiply_fusion = f32[8,1024]{1,0:T(8,128)S(1)} fusion(pred[8,1024]{1,0:T(8,128)(4,1)S(1)} %get-tuple-element.13, pred[8,1024]{1,0:T(8,128)(4,1)S(1)} %get-tuple-element.12, pred[8,1024]{1,0:T(8,128)(4,1)S(1)} %get-tuple-element.11, pred[8,1024]{1,0:T(8,128)(4,1)S(1)} %get-tuple-element.10, pred[8,1024]{1,0:T(8,128)(4,1)S(1)} %get-tuple-element.9, ...), kind=kLoop, calls=%fused_computation.59 | loop fusion | flops 131072 | bytes 98336 | tf_op jit(solution)/shard_map/mul | solution.py:33
  27.8 5.0 %add_multiply_fusion.1 = f32[8,1024]{1,0:T(8,128)S(1)} fusion(pred[8,1024]{1,0:T(8,128)(4,1)S(1)} %get-tuple-element.13, pred[8,1024]{1,0:T(8,128)(4,1)S(1)} %get-tuple-element.12, pred[8,1024]{1,0:T(8,128)(4,1)S(1)} %get-tuple-element.11, pred[8,1024]{1,0:T(8,128)(4,1)S(1)} %get-tuple-element.10, pred[8,1024]{1,0:T(8,128)(4,1)S(1)} %get-tuple-element.9, ...), kind=kLoop, calls=%fused_computation.60 | loop fusion | flops 131072 | bytes 98336 | tf_op jit(solution)/shard_map/mul | solution.py:32
  33.7 1.3 collective-permute-start.2
  35.0 5.4 %collective-permute-start.3 = (f32[32,1,1024]{2,0,1:T(8,128)S(1)}, f32[32,1,1024]{2,0,1:T(8,128)S(1)}, u32[]{:S(2)}, u32[]{:S(2)}) collective-permute-start(f32[32,1,1024]{2,0,1:T(8,128)S(1)} %get-tuple-element.38), channel_id=1, source_target_pairs={{0,4},{4,8},{8,12},{12,16},{16,20},{20,24},{24,28},{1,5},{5,9},{9,... | collective-permute-start | bytes 393224 | tf_op jit(solution)/shard_map/ppermute | solution.py:16
  41.4 2.9 collective-permute-done.3
  45.1 1.3 collective-permute-start.4
  46.4 5.0 %collective-permute-start.5 = (f32[32,1,1024]{2,0,1:T(8,128)S(1)}, f32[32,1,1024]{2,0,1:T(8,128)S(1)}, u32[]{:S(2)}, u32[]{:S(2)}) collective-permute-start(f32[32,1,1024]{2,0,1:T(8,128)S(1)} %get-tuple-element.34), channel_id=1, source_target_pairs={{0,4},{4,8},{8,12},{12,16},{16,20},{20,24},{24,28},{1,5},{5,9},{9,... | collective-permute-start | bytes 393224 | tf_op jit(solution)/shard_map/ppermute | solution.py:16
  52.9 3.0 collective-permute-done.5
  56.5 1.3 collective-permute-start.6
  57.8 5.0 %collective-permute-start.7 = (f32[32,1,1024]{2,0,1:T(8,128)S(1)}, f32[32,1,1024]{2,0,1:T(8,128)S(1)}, u32[]{:S(2)}, u32[]{:S(2)}) collective-permute-start(f32[32,1,1024]{2,0,1:T(8,128)S(1)} %get-tuple-element.30), channel_id=1, source_target_pairs={{0,4},{4,8},{8,12},{12,16},{16,20},{20,24},{24,28},{1,5},{5,9},{9,... | collective-permute-start | bytes 393224 | tf_op jit(solution)/shard_map/ppermute | solution.py:16
  63.3 1.3 collective-permute-done.6
  64.6 3.0 collective-permute-done.7
  68.2 1.3 collective-permute-start.8
  69.5 5.0 %collective-permute-start.9 = (f32[32,1,1024]{2,0,1:T(8,128)S(1)}, f32[32,1,1024]{2,0,1:T(8,128)S(1)}, u32[]{:S(2)}, u32[]{:S(2)}) collective-permute-start(f32[32,1,1024]{2,0,1:T(8,128)S(1)} %get-tuple-element.26), channel_id=1, source_target_pairs={{0,4},{4,8},{8,12},{12,16},{16,20},{20,24},{24,28},{1,5},{5,9},{9,... | collective-permute-start | bytes 393224 | tf_op jit(solution)/shard_map/ppermute | solution.py:16
  75.0 1.3 collective-permute-done.8
  76.3 3.0 collective-permute-done.9
  80.0 1.3 collective-permute-start.10
  81.3 5.0 %collective-permute-start.11 = (f32[32,1,1024]{2,0,1:T(8,128)S(1)}, f32[32,1,1024]{2,0,1:T(8,128)S(1)}, u32[]{:S(2)}, u32[]{:S(2)}) collective-permute-start(f32[32,1,1024]{2,0,1:T(8,128)S(1)} %get-tuple-element.22), channel_id=1, source_target_pairs={{0,4},{4,8},{8,12},{12,16},{16,20},{20,24},{24,28},{1,5},{5,9},{9,... | collective-permute-start | bytes 393224 | tf_op jit(solution)/shard_map/ppermute | solution.py:16
  86.7 1.3 collective-permute-done.10
  88.0 3.0 collective-permute-done.11
  91.7 1.3 collective-permute-start.12
  93.0 5.0 %collective-permute-start.13 = (f32[32,1,1024]{2,0,1:T(8,128)S(1)}, f32[32,1,1024]{2,0,1:T(8,128)S(1)}, u32[]{:S(2)}, u32[]{:S(2)}) collective-permute-start(f32[32,1,1024]{2,0,1:T(8,128)S(1)} %get-tuple-element.18), channel_id=1, source_target_pairs={{0,4},{4,8},{8,12},{12,16},{16,20},{20,24},{24,28},{1,5},{5,9},{9,... | collective-permute-start | bytes 393224 | tf_op jit(solution)/shard_map/ppermute | solution.py:16
  98.4 1.3 collective-permute-done.12
  99.7 3.0 collective-permute-done.13
  103.4 1.3 collective-permute-start.14
  104.7 5.0 %collective-permute-start.15 = (f32[32,1,1024]{2,0,1:T(8,128)S(1)}, f32[32,1,1024]{2,0,1:T(8,128)S(1)}, u32[]{:S(2)}, u32[]{:S(2)}) collective-permute-start(f32[32,1,1024]{2,0,1:T(8,128)S(1)} %get-tuple-element.14), channel_id=1, source_target_pairs={{0,4},{4,8},{8,12},{12,16},{16,20},{20,24},{24,28},{1,5},{5,9},{9,... | collective-permute-start | bytes 393224 | tf_op jit(solution)/shard_map/ppermute | solution.py:16
  110.1 1.3 collective-permute-done.14
  111.5 3.0 collective-permute-done.15
  115.1 2.6 copy.43
  117.7 2.8 gather_fusion
  121.4 3.4 %all-to-all-start = ((f32[4,1,1024]{2,1,0:T(1,128)}), f32[4,1,1024]{2,1,0:T(1,128)S(1)}, u32[]{:S(2)}, u32[]{:S(2)}) async-start(f32[4,1,1024]{2,1,0:T(1,128)} %reshape.69), calls=%async_computation | async-start | bytes 32768 | tf_op jit(solution)/shard_map/all_to_all | solution.py:92
  124.9 2.7 copy.46
  127.6 4.8 %reshape.67 = f32[4,1,65536]{2,1,0:T(1,128)} reshape(f32[1024,8,32]{2,1,0:T(8,128)} %bitcast.117) | data formatting | bytes 2097152
  132.4 3.5 %all-to-all-start.1 = ((f32[4,1,65536]{2,1,0:T(1,128)}), f32[4,1,65536]{2,1,0:T(1,128)S(1)}, u32[]{:S(2)}, u32[]{:S(2)}) async-start(f32[4,1,65536]{2,1,0:T(1,128)} %reshape.67), calls=%async_computation.1 | async-start | bytes 2097152 | tf_op jit(solution)/shard_map/all_to_all | solution.py:116
  139.1 44.7 %psum.15 = f32[128]{0:T(128)S(1)} all-reduce(f32[128]{0:T(128)S(1)} %convolution_bitcast_fusion.2), channel_id=1, replica_groups=mesh['slab'=8,'mem'=4] {'slab','mem'}, use_global_device_ids=true, to_apply=%region_3.4 | all-reduce | flops 128 | bytes 1024 | tf_op jit(solution)/shard_map/psum | solution.py:97
  183.8 76.2 %all-reduce.18.cloned.1.call-done = f32[128,128]{1,0:T(8,128)} async-done(((f32[128,128]{1,0:T(8,128)}), f32[128,128]{1,0:T(8,128)}) %all-reduce.18.cloned.1.call-update) | async-done | bytes 65552 | tf_op jit(solution)/shard_map/psum | solution.py:97
  259.9 1.5 select_reduce_fusion
  261.4 1.6 fusion.7
  263.2 1.6 fusion.17
  270.8 3.7 %reduce.2 = f32[4,65536]{1,0:T(4,128)S(1)} reduce(f32[4,1,65536]{2,1,0:T(1,128)S(1)} %all-to-all-done.1, f32[]{:T(128)} %broadcast.130), dimensions={1}, to_apply=%all_to_all.41.reduce_sub_computation | reduce | bytes 2097156 | tf_op jit(solution)/shard_map/all_to_all | solution.py:116
  274.5 3.4 %reshape.68 = f32[1024,8,32]{2,1,0:T(8,128)} reshape(f32[4,65536]{1,0:T(4,128)S(1)} %reduce.2) | data formatting | bytes 2097152
  277.9 2.8 copy.47
  282.4 18.2 %all_to_all.52 = f32[128,8,256]{2,1,0:T(8,128)S(1)} all-to-all(f32[128,8,256]{2,1,0:T(8,128)S(1)} %copy.49), channel_id=1, replica_groups=mesh['slab'=8,'mem'=4] {'mem'}, dimensions={0} | all-to-all | bytes 2097152 | tf_op jit(solution)/shard_map/all_to_all | solution.py:119
  300.6 1.1 copy.50
  (96 shorter events, 22.8 us)
Async XLA Ops:
  6.5 9.8 %copy-start.2 = (f32[8]{0:T(128)S(1)}, f32[8]{0:T(128)}, u32[]{:S(2)}) copy-start(f32[8]{0:T(128)} %param.11) | copy-start | bytes 100
  6.5 10.5 %copy-start = (f32[2,8]{1,0:T(2,128)S(1)}, f32[2,8]{1,0:T(2,128)}, u32[]{:S(2)}) copy-start(f32[2,8]{1,0:T(2,128)} %param.12) | copy-start | bytes 196
  6.5 11.2 %copy-start.5 = (s32[128]{0:T(128)S(1)}, s32[128]{0:T(128)}, u32[]{:S(2)}) copy-start(s32[128]{0:T(128)} %param.13) | copy-start | bytes 1540
  6.5 11.2 %copy-start.3 = (s32[8,1024]{1,0:T(8,128)S(1)}, s32[8,1024]{1,0:T(8,128)}, u32[]{:S(2)}) copy-start(s32[8,1024]{1,0:T(8,128)} %param.10) | copy-start | bytes 98308
  6.5 26.3 %copy-start.1 = (s32[8,1024]{1,0:T(8,128)S(1)}, s32[8,1024]{1,0:T(8,128)}, u32[]{:S(2)}) copy-start(s32[8,1024]{1,0:T(8,128)} %param.9) | copy-start | bytes 98308
  9.2 23.8 %collective-permute-start = (f32[32,1,1024]{2,0,1:T(8,128)}, f32[32,1,1024]{2,0,1:T(8,128)S(1)}, u32[]{:S(2)}, u32[]{:S(2)}) collective-permute-start(f32[32,1,1024]{2,0,1:T(8,128)} %get-tuple-element.43), channel_id=1, source_target_pairs={{4,0},{8,4},{12,8},{16,12},{20,16},{24,20},{28,24},{5,1},{9,5},{13... | collective-permute-start | bytes 393224 | tf_op jit(solution)/shard_map/ppermute | solution.py:19
  10.5 22.5 %collective-permute-start.1 = (f32[32,1,1024]{2,0,1:T(8,128)}, f32[32,1,1024]{2,0,1:T(8,128)S(1)}, u32[]{:S(2)}, u32[]{:S(2)}) collective-permute-start(f32[32,1,1024]{2,0,1:T(8,128)} %get-tuple-element.42), channel_id=1, source_target_pairs={{0,4},{4,8},{8,12},{12,16},{16,20},{20,24},{24,28},{1,5},{5,9},{9,... | collective-permute-start | bytes 393224 | tf_op jit(solution)/shard_map/ppermute | solution.py:16
  33.7 7.8 %collective-permute-start.2 = (f32[32,1,1024]{2,0,1:T(8,128)S(1)}, f32[32,1,1024]{2,0,1:T(8,128)S(1)}, u32[]{:S(2)}, u32[]{:S(2)}) collective-permute-start(f32[32,1,1024]{2,0,1:T(8,128)S(1)} %get-tuple-element.39), channel_id=1, source_target_pairs={{4,0},{8,4},{12,8},{16,12},{20,16},{24,20},{28,24},{5,1},{9,5},{13... | collective-permute-start | bytes 393224 | tf_op jit(solution)/shard_map/ppermute | solution.py:19
  35.0 9.4 %collective-permute-start.3 = (f32[32,1,1024]{2,0,1:T(8,128)S(1)}, f32[32,1,1024]{2,0,1:T(8,128)S(1)}, u32[]{:S(2)}, u32[]{:S(2)}) collective-permute-start(f32[32,1,1024]{2,0,1:T(8,128)S(1)} %get-tuple-element.38), channel_id=1, source_target_pairs={{0,4},{4,8},{8,12},{12,16},{16,20},{20,24},{24,28},{1,5},{5,9},{9,... | collective-permute-start | bytes 393224 | tf_op jit(solution)/shard_map/ppermute | solution.py:16
  45.1 7.8 %collective-permute-start.4 = (f32[32,1,1024]{2,0,1:T(8,128)S(1)}, f32[32,1,1024]{2,0,1:T(8,128)S(1)}, u32[]{:S(2)}, u32[]{:S(2)}) collective-permute-start(f32[32,1,1024]{2,0,1:T(8,128)S(1)} %get-tuple-element.35), channel_id=1, source_target_pairs={{4,0},{8,4},{12,8},{16,12},{20,16},{24,20},{28,24},{5,1},{9,5},{13... | collective-permute-start | bytes 393224 | tf_op jit(solution)/shard_map/ppermute | solution.py:19
  46.4 9.5 %collective-permute-start.5 = (f32[32,1,1024]{2,0,1:T(8,128)S(1)}, f32[32,1,1024]{2,0,1:T(8,128)S(1)}, u32[]{:S(2)}, u32[]{:S(2)}) collective-permute-start(f32[32,1,1024]{2,0,1:T(8,128)S(1)} %get-tuple-element.34), channel_id=1, source_target_pairs={{0,4},{4,8},{8,12},{12,16},{16,20},{20,24},{24,28},{1,5},{5,9},{9,... | collective-permute-start | bytes 393224 | tf_op jit(solution)/shard_map/ppermute | solution.py:16
  56.5 8.1 %collective-permute-start.6 = (f32[32,1,1024]{2,0,1:T(8,128)S(1)}, f32[32,1,1024]{2,0,1:T(8,128)S(1)}, u32[]{:S(2)}, u32[]{:S(2)}) collective-permute-start(f32[32,1,1024]{2,0,1:T(8,128)S(1)} %get-tuple-element.31), channel_id=1, source_target_pairs={{4,0},{8,4},{12,8},{16,12},{20,16},{24,20},{28,24},{5,1},{9,5},{13... | collective-permute-start | bytes 393224 | tf_op jit(solution)/shard_map/ppermute | solution.py:19
  57.8 9.7 %collective-permute-start.7 = (f32[32,1,1024]{2,0,1:T(8,128)S(1)}, f32[32,1,1024]{2,0,1:T(8,128)S(1)}, u32[]{:S(2)}, u32[]{:S(2)}) collective-permute-start(f32[32,1,1024]{2,0,1:T(8,128)S(1)} %get-tuple-element.30), channel_id=1, source_target_pairs={{0,4},{4,8},{8,12},{12,16},{16,20},{20,24},{24,28},{1,5},{5,9},{9,... | collective-permute-start | bytes 393224 | tf_op jit(solution)/shard_map/ppermute | solution.py:16
  68.2 8.1 %collective-permute-start.8 = (f32[32,1,1024]{2,0,1:T(8,128)S(1)}, f32[32,1,1024]{2,0,1:T(8,128)S(1)}, u32[]{:S(2)}, u32[]{:S(2)}) collective-permute-start(f32[32,1,1024]{2,0,1:T(8,128)S(1)} %get-tuple-element.27), channel_id=1, source_target_pairs={{4,0},{8,4},{12,8},{16,12},{20,16},{24,20},{28,24},{5,1},{9,5},{13... | collective-permute-start | bytes 393224 | tf_op jit(solution)/shard_map/ppermute | solution.py:19
  69.5 9.7 %collective-permute-start.9 = (f32[32,1,1024]{2,0,1:T(8,128)S(1)}, f32[32,1,1024]{2,0,1:T(8,128)S(1)}, u32[]{:S(2)}, u32[]{:S(2)}) collective-permute-start(f32[32,1,1024]{2,0,1:T(8,128)S(1)} %get-tuple-element.26), channel_id=1, source_target_pairs={{0,4},{4,8},{8,12},{12,16},{16,20},{20,24},{24,28},{1,5},{5,9},{9,... | collective-permute-start | bytes 393224 | tf_op jit(solution)/shard_map/ppermute | solution.py:16
  80.0 8.1 %collective-permute-start.10 = (f32[32,1,1024]{2,0,1:T(8,128)S(1)}, f32[32,1,1024]{2,0,1:T(8,128)S(1)}, u32[]{:S(2)}, u32[]{:S(2)}) collective-permute-start(f32[32,1,1024]{2,0,1:T(8,128)S(1)} %get-tuple-element.23), channel_id=1, source_target_pairs={{4,0},{8,4},{12,8},{16,12},{20,16},{24,20},{28,24},{5,1},{9,5},{13... | collective-permute-start | bytes 393224 | tf_op jit(solution)/shard_map/ppermute | solution.py:19
  81.3 9.7 %collective-permute-start.11 = (f32[32,1,1024]{2,0,1:T(8,128)S(1)}, f32[32,1,1024]{2,0,1:T(8,128)S(1)}, u32[]{:S(2)}, u32[]{:S(2)}) collective-permute-start(f32[32,1,1024]{2,0,1:T(8,128)S(1)} %get-tuple-element.22), channel_id=1, source_target_pairs={{0,4},{4,8},{8,12},{12,16},{16,20},{20,24},{24,28},{1,5},{5,9},{9,... | collective-permute-start | bytes 393224 | tf_op jit(solution)/shard_map/ppermute | solution.py:16
  91.7 8.1 %collective-permute-start.12 = (f32[32,1,1024]{2,0,1:T(8,128)S(1)}, f32[32,1,1024]{2,0,1:T(8,128)S(1)}, u32[]{:S(2)}, u32[]{:S(2)}) collective-permute-start(f32[32,1,1024]{2,0,1:T(8,128)S(1)} %get-tuple-element.19), channel_id=1, source_target_pairs={{4,0},{8,4},{12,8},{16,12},{20,16},{24,20},{28,24},{5,1},{9,5},{13... | collective-permute-start | bytes 393224 | tf_op jit(solution)/shard_map/ppermute | solution.py:19
  93.0 9.7 %collective-permute-start.13 = (f32[32,1,1024]{2,0,1:T(8,128)S(1)}, f32[32,1,1024]{2,0,1:T(8,128)S(1)}, u32[]{:S(2)}, u32[]{:S(2)}) collective-permute-start(f32[32,1,1024]{2,0,1:T(8,128)S(1)} %get-tuple-element.18), channel_id=1, source_target_pairs={{0,4},{4,8},{8,12},{12,16},{16,20},{20,24},{24,28},{1,5},{5,9},{9,... | collective-permute-start | bytes 393224 | tf_op jit(solution)/shard_map/ppermute | solution.py:16
  103.4 8.1 %collective-permute-start.14 = (f32[32,1,1024]{2,0,1:T(8,128)S(1)}, f32[32,1,1024]{2,0,1:T(8,128)S(1)}, u32[]{:S(2)}, u32[]{:S(2)}) collective-permute-start(f32[32,1,1024]{2,0,1:T(8,128)S(1)} %get-tuple-element.15), channel_id=1, source_target_pairs={{4,0},{8,4},{12,8},{16,12},{20,16},{24,20},{28,24},{5,1},{9,5},{13... | collective-permute-start | bytes 393224 | tf_op jit(solution)/shard_map/ppermute | solution.py:19
  104.7 9.7 %collective-permute-start.15 = (f32[32,1,1024]{2,0,1:T(8,128)S(1)}, f32[32,1,1024]{2,0,1:T(8,128)S(1)}, u32[]{:S(2)}, u32[]{:S(2)}) collective-permute-start(f32[32,1,1024]{2,0,1:T(8,128)S(1)} %get-tuple-element.14), channel_id=1, source_target_pairs={{0,4},{4,8},{8,12},{12,16},{16,20},{20,24},{24,28},{1,5},{5,9},{9,... | collective-permute-start | bytes 393224 | tf_op jit(solution)/shard_map/ppermute | solution.py:16
  114.4 10.4 %copy-start.4 = (f32[128]{0:T(128)S(1)}, f32[128]{0:T(128)}, u32[]{:S(2)}) copy-start(f32[128]{0:T(128)} %param.15) | copy-start | bytes 1540
  121.4 11.1 %all-to-all-start = ((f32[4,1,1024]{2,1,0:T(1,128)}), f32[4,1,1024]{2,1,0:T(1,128)S(1)}, u32[]{:S(2)}, u32[]{:S(2)}) async-start(f32[4,1,1024]{2,1,0:T(1,128)} %reshape.69), calls=%async_computation | async-start | bytes 32768 | tf_op jit(solution)/shard_map/all_to_all | solution.py:92
  127.6 11.3 %copy-start.6 = (f32[128]{0:T(128)S(1)}, f32[128]{0:T(128)}, u32[]{:S(2)}) copy-start(f32[128]{0:T(128)} %param.14) | copy-start | bytes 1540
  132.4 138.3 %all-to-all-start.1 = ((f32[4,1,65536]{2,1,0:T(1,128)}), f32[4,1,65536]{2,1,0:T(1,128)S(1)}, u32[]{:S(2)}, u32[]{:S(2)}) async-start(f32[4,1,65536]{2,1,0:T(1,128)} %reshape.67), calls=%async_computation.1 | async-start | bytes 2097152 | tf_op jit(solution)/shard_map/all_to_all | solution.py:116
  136.0 124.0 %all-reduce.18.cloned.1.call-start = ((), (), s32[]{:S(2)}) async-start(), calls=%async_computation.3 | async-start | bytes 131072 | tf_op jit(solution)/shard_map/psum | solution.py:97
Sparse Core Ops, SparseCore 0:
  142.4 117.4 all-reduce.17
where the time goes:
time: 310 us; the launch traced here: 309 us
  waiting for transfers between devices  105 us (34%)
  blocking collectives  62.9 us (20%)
  starting transfers between devices  58.4 us (19%)
  local copies, waits for them, and re-layouts  29.9 us (10%)
  other arithmetic  26.7 us (9%)
  between operations  15.3 us (5%)
  matrix products  10.1 us (3%)
    psum x1, waiting for transfers between devices, local(): gram, proj = lax.psum((gram_part, proj_part), ('slab', 'mem'))  76.2 us
    psum x1, blocking collectives, local(): gram, proj = lax.psum((gram_part, proj_part), ('slab', 'mem'))  44.7 us
    ppermute x8, starting transfers between devices, extended(): lax.ppermute(lax.slice_in_dim(block, block.shape[dim] - width, None, axis...  41.1 us
    ppermute x8, waiting for transfers between devices, extended(): lax.ppermute(lax.slice_in_dim(block, block.shape[dim] - width, None, axis...  20.7 us
    all_to_all x1, blocking collectives, local(): return lax.all_to_all(mixed, 'mem', split_axis=0, concat_axis=2, tiled=True)  18.2 us
    unnamed x19, local copies, waits for them, and re-layouts  10.9 us
    ppermute x8, starting transfers between devices, extended(): lax.ppermute(lax.slice_in_dim(block, 0, width, axis=dim), axis, backward)  10.3 us
    ppermute x8, waiting for transfers between devices, extended(): lax.ppermute(lax.slice_in_dim(block, 0, width, axis=dim), axis, backward)  8.4 us
  transfers between devices with their start and end apart: 19, of which 15 were waited for; matrix products, arithmetic and copies ran while one was open for 13% of the time, Pallas kernels for 0%

commit v1 on v0

--- a/solution.py
+++ b/solution.py
@@ -94,7 +94,7 @@
     values = lax.dynamic_slice_in_dim(obs_values, member_group * count, count)
     variances = lax.dynamic_slice_in_dim(obs_var, member_group * count, count)
     gram_part, proj_part = statistics(columns, values, variances, factor, ens_total)
-    gram, proj = lax.psum((gram_part, proj_part), ("slab", "mem"))
+    gram, proj = lax.psum(lax.psum((gram_part, proj_part), axis_name="mem"), axis_name="slab")
     ident = jnp.eye(ens_total, dtype=jnp.float32)
     matrix = ident + gram
     scale = jnp.trace(matrix)

time: 310 us -> 292 us (0.942)
  blocking collectives: 62.9 us -> 44.2 us
    psum x1 -> x2, blocking collectives: 44.7 us -> 27.2 us  [the longest x1 21.5 us: local(): lax.psum(lax.psum((gram_part, proj_part), axis_name='mem'), axis_name='sl...]
    psum x1 -> x2, waiting for transfers between devices: 76.2 us -> 76.3 us  [the longest x1 44.9 us: local(): lax.psum(lax.psum((gram_part, proj_part), axis_name='mem'), axis_name='sl...]
  transfers between devices with their start and end apart: 19 -> 20, of which waited for: 15 -> 16; matrix products, arithmetic and copies ran while one was open for 13% -> 14% of each run, Pallas kernels for 0% -> 0%
where the time goes in v1:
time: 292 us; the launch traced here: 290 us
  waiting for transfers between devices  105 us (36%)
  starting transfers between devices  58.4 us (20%)
  blocking collectives  44.2 us (15%)
  local copies, waits for them, and re-layouts  29.9 us (10%)
  other arithmetic  26.6 us (9%)
  between operations  15.5 us (5%)
  matrix products  10.3 us (4%)
    psum x1, waiting for transfers between devices, local(): lax.psum(lax.psum((gram_part, proj_part), axis_name='mem'), axis_name='sl...  44.9 us
    ppermute x8, starting transfers between devices, extended(): lax.ppermute(lax.slice_in_dim(block, block.shape[dim] - width, None, axis...  41.1 us
    psum x1, waiting for transfers between devices, local(): lax.psum((gram_part, proj_part), axis_name='mem')  31.4 us
    psum x1, blocking collectives, local(): lax.psum(lax.psum((gram_part, proj_part), axis_name='mem'), axis_name='sl...  21.5 us
    ppermute x8, waiting for transfers between devices, extended(): lax.ppermute(lax.slice_in_dim(block, block.shape[dim] - width, None, axis...  20.7 us
    all_to_all x1, blocking collectives, local(): return lax.all_to_all(mixed, 'mem', split_axis=0, concat_axis=2, tiled=True)  17 us
    unnamed x19, local copies, waits for them, and re-layouts  10.9 us
    ppermute x8, starting transfers between devices, extended(): lax.ppermute(lax.slice_in_dim(block, 0, width, axis=dim), axis, backward)  10.3 us
  transfers between devices with their start and end apart: 20, of which 16 were waited for; matrix products, arithmetic and copies ran while one was open for 14% of the time, Pallas kernels for 0%

profile of v1, /device:TPU:0, one launch (start us, length us, event | category | flops | bytes accessed | tf_op | source)
XLA Modules:
  0.0 290.4 jit_solution(12560306184917314220)
XLA Ops:
  6.5 1.9 copy.42
  10.4 5.5 %collective-permute-start.1 = (f32[32,1,1024]{2,0,1:T(8,128)}, f32[32,1,1024]{2,0,1:T(8,128)S(1)}, u32[]{:S(2)}, u32[]{:S(2)}) collective-permute-start(f32[32,1,1024]{2,0,1:T(8,128)} %get-tuple-element.42), channel_id=1, source_target_pairs={{0,4},{4,8},{8,12},{12,16},{16,20},{20,24},{24,28},{1,5},{5,9},{9,... | collective-permute-start | bytes 393224 | tf_op jit(solution)/shard_map/ppermute | solution.py:16
  17.7 5.0 %select_add_fusion = (f32[8,1024]{1,0:T(8,128)S(1)}, pred[8,1024]{1,0:T(8,128)(4,1)S(1)}, pred[8,1024]{1,0:T(8,128)(4,1)S(1)}, pred[8,1024]{1,0:T(8,128)(4,1)S(1...) fusion(f32[]{:T(128)} %bitcast.7, f32[]{:T(128)} %bitcast.6, ...), kind=kLoop, calls=%fused_computation.61 | loop fusion | flops 188416 | bytes 131104 | tf_op jit(solution)/shard_map/add | solution.py:43
  22.8 5.0 %add_multiply_fusion = f32[8,1024]{1,0:T(8,128)S(1)} fusion(pred[8,1024]{1,0:T(8,128)(4,1)S(1)} %get-tuple-element.13, pred[8,1024]{1,0:T(8,128)(4,1)S(1)} %get-tuple-element.12, pred[8,1024]{1,0:T(8,128)(4,1)S(1)} %get-tuple-element.11, pred[8,1024]{1,0:T(8,128)(4,1)S(1)} %get-tuple-element.10, pred[8,1024]{1,0:T(8,128)(4,1)S(1)} %get-tuple-element.9, ...), kind=kLoop, calls=%fused_computation.59 | loop fusion | flops 131072 | bytes 98336 | tf_op jit(solution)/shard_map/mul | solution.py:33
  27.7 5.0 %add_multiply_fusion.1 = f32[8,1024]{1,0:T(8,128)S(1)} fusion(pred[8,1024]{1,0:T(8,128)(4,1)S(1)} %get-tuple-element.13, pred[8,1024]{1,0:T(8,128)(4,1)S(1)} %get-tuple-element.12, pred[8,1024]{1,0:T(8,128)(4,1)S(1)} %get-tuple-element.11, pred[8,1024]{1,0:T(8,128)(4,1)S(1)} %get-tuple-element.10, pred[8,1024]{1,0:T(8,128)(4,1)S(1)} %get-tuple-element.9, ...), kind=kLoop, calls=%fused_computation.60 | loop fusion | flops 131072 | bytes 98336 | tf_op jit(solution)/shard_map/mul | solution.py:32
  33.5 1.3 collective-permute-start.2
  34.8 5.4 %collective-permute-start.3 = (f32[32,1,1024]{2,0,1:T(8,128)S(1)}, f32[32,1,1024]{2,0,1:T(8,128)S(1)}, u32[]{:S(2)}, u32[]{:S(2)}) collective-permute-start(f32[32,1,1024]{2,0,1:T(8,128)S(1)} %get-tuple-element.38), channel_id=1, source_target_pairs={{0,4},{4,8},{8,12},{12,16},{16,20},{20,24},{24,28},{1,5},{5,9},{9,... | collective-permute-start | bytes 393224 | tf_op jit(solution)/shard_map/ppermute | solution.py:16
  41.3 2.9 %collective-permute-done.3 = f32[32,1,1024]{2,0,1:T(8,128)S(1)} collective-permute-done((f32[32,1,1024]{2,0,1:T(8,128)S(1)}, f32[32,1,1024]{2,0,1:T(8,128)S(1)}, u32[]{:S(2)}, u32[]{:S(2)}) %collective-permute-start.3) | collective-permute-done | bytes 131104 | tf_op jit(solution)/shard_map/ppermute | solution.py:16
  44.9 1.3 collective-permute-start.4
  46.2 5.0 %collective-permute-start.5 = (f32[32,1,1024]{2,0,1:T(8,128)S(1)}, f32[32,1,1024]{2,0,1:T(8,128)S(1)}, u32[]{:S(2)}, u32[]{:S(2)}) collective-permute-start(f32[32,1,1024]{2,0,1:T(8,128)S(1)} %get-tuple-element.34), channel_id=1, source_target_pairs={{0,4},{4,8},{8,12},{12,16},{16,20},{20,24},{24,28},{1,5},{5,9},{9,... | collective-permute-start | bytes 393224 | tf_op jit(solution)/shard_map/ppermute | solution.py:16
  52.7 3.0 %collective-permute-done.5 = f32[32,1,1024]{2,0,1:T(8,128)S(1)} collective-permute-done((f32[32,1,1024]{2,0,1:T(8,128)S(1)}, f32[32,1,1024]{2,0,1:T(8,128)S(1)}, u32[]{:S(2)}, u32[]{:S(2)}) %collective-permute-start.5) | collective-permute-done | bytes 131104 | tf_op jit(solution)/shard_map/ppermute | solution.py:16
  56.4 1.3 collective-permute-start.6
  57.7 5.0 %collective-permute-start.7 = (f32[32,1,1024]{2,0,1:T(8,128)S(1)}, f32[32,1,1024]{2,0,1:T(8,128)S(1)}, u32[]{:S(2)}, u32[]{:S(2)}) collective-permute-start(f32[32,1,1024]{2,0,1:T(8,128)S(1)} %get-tuple-element.30), channel_id=1, source_target_pairs={{0,4},{4,8},{8,12},{12,16},{16,20},{20,24},{24,28},{1,5},{5,9},{9,... | collective-permute-start | bytes 393224 | tf_op jit(solution)/shard_map/ppermute | solution.py:16
  63.1 1.3 collective-permute-done.6
  64.4 3.0 %collective-permute-done.7 = f32[32,1,1024]{2,0,1:T(8,128)S(1)} collective-permute-done((f32[32,1,1024]{2,0,1:T(8,128)S(1)}, f32[32,1,1024]{2,0,1:T(8,128)S(1)}, u32[]{:S(2)}, u32[]{:S(2)}) %collective-permute-start.7) | collective-permute-done | bytes 131104 | tf_op jit(solution)/shard_map/ppermute | solution.py:16
  68.1 1.3 collective-permute-start.8
  69.4 5.0 %collective-permute-start.9 = (f32[32,1,1024]{2,0,1:T(8,128)S(1)}, f32[32,1,1024]{2,0,1:T(8,128)S(1)}, u32[]{:S(2)}, u32[]{:S(2)}) collective-permute-start(f32[32,1,1024]{2,0,1:T(8,128)S(1)} %get-tuple-element.26), channel_id=1, source_target_pairs={{0,4},{4,8},{8,12},{12,16},{16,20},{20,24},{24,28},{1,5},{5,9},{9,... | collective-permute-start | bytes 393224 | tf_op jit(solution)/shard_map/ppermute | solution.py:16
  74.8 1.3 collective-permute-done.8
  76.2 3.0 %collective-permute-done.9 = f32[32,1,1024]{2,0,1:T(8,128)S(1)} collective-permute-done((f32[32,1,1024]{2,0,1:T(8,128)S(1)}, f32[32,1,1024]{2,0,1:T(8,128)S(1)}, u32[]{:S(2)}, u32[]{:S(2)}) %collective-permute-start.9) | collective-permute-done | bytes 131104 | tf_op jit(solution)/shard_map/ppermute | solution.py:16
  79.8 1.3 collective-permute-start.10
  81.1 5.0 %collective-permute-start.11 = (f32[32,1,1024]{2,0,1:T(8,128)S(1)}, f32[32,1,1024]{2,0,1:T(8,128)S(1)}, u32[]{:S(2)}, u32[]{:S(2)}) collective-permute-start(f32[32,1,1024]{2,0,1:T(8,128)S(1)} %get-tuple-element.22), channel_id=1, source_target_pairs={{0,4},{4,8},{8,12},{12,16},{16,20},{20,24},{24,28},{1,5},{5,9},{9,... | collective-permute-start | bytes 393224 | tf_op jit(solution)/shard_map/ppermute | solution.py:16
  86.5 1.3 collective-permute-done.10
  87.9 3.0 %collective-permute-done.11 = f32[32,1,1024]{2,0,1:T(8,128)S(1)} collective-permute-done((f32[32,1,1024]{2,0,1:T(8,128)S(1)}, f32[32,1,1024]{2,0,1:T(8,128)S(1)}, u32[]{:S(2)}, u32[]{:S(2)}) %collective-permute-start.11) | collective-permute-done | bytes 131104 | tf_op jit(solution)/shard_map/ppermute | solution.py:16
  91.5 1.3 collective-permute-start.12
  92.8 5.0 %collective-permute-start.13 = (f32[32,1,1024]{2,0,1:T(8,128)S(1)}, f32[32,1,1024]{2,0,1:T(8,128)S(1)}, u32[]{:S(2)}, u32[]{:S(2)}) collective-permute-start(f32[32,1,1024]{2,0,1:T(8,128)S(1)} %get-tuple-element.18), channel_id=1, source_target_pairs={{0,4},{4,8},{8,12},{12,16},{16,20},{20,24},{24,28},{1,5},{5,9},{9,... | collective-permute-start | bytes 393224 | tf_op jit(solution)/shard_map/ppermute | solution.py:16
  98.3 1.3 collective-permute-done.12
  99.6 3.0 %collective-permute-done.13 = f32[32,1,1024]{2,0,1:T(8,128)S(1)} collective-permute-done((f32[32,1,1024]{2,0,1:T(8,128)S(1)}, f32[32,1,1024]{2,0,1:T(8,128)S(1)}, u32[]{:S(2)}, u32[]{:S(2)}) %collective-permute-start.13) | collective-permute-done | bytes 131104 | tf_op jit(solution)/shard_map/ppermute | solution.py:16
  103.3 1.3 collective-permute-start.14
  104.6 5.0 %collective-permute-start.15 = (f32[32,1,1024]{2,0,1:T(8,128)S(1)}, f32[32,1,1024]{2,0,1:T(8,128)S(1)}, u32[]{:S(2)}, u32[]{:S(2)}) collective-permute-start(f32[32,1,1024]{2,0,1:T(8,128)S(1)} %get-tuple-element.14), channel_id=1, source_target_pairs={{0,4},{4,8},{8,12},{12,16},{16,20},{20,24},{24,28},{1,5},{5,9},{9,... | collective-permute-start | bytes 393224 | tf_op jit(solution)/shard_map/ppermute | solution.py:16
  110.0 1.3 collective-permute-done.14
  111.3 3.0 %collective-permute-done.15 = f32[32,1,1024]{2,0,1:T(8,128)S(1)} collective-permute-done((f32[32,1,1024]{2,0,1:T(8,128)S(1)}, f32[32,1,1024]{2,0,1:T(8,128)S(1)}, u32[]{:S(2)}, u32[]{:S(2)}) %collective-permute-start.15) | collective-permute-done | bytes 131104 | tf_op jit(solution)/shard_map/ppermute | solution.py:16
  115.0 2.6 copy.43
  117.6 2.8 gather_fusion
  121.2 3.4 %all-to-all-start = ((f32[4,1,1024]{2,1,0:T(1,128)}), f32[4,1,1024]{2,1,0:T(1,128)S(1)}, u32[]{:S(2)}, u32[]{:S(2)}) async-start(f32[4,1,1024]{2,1,0:T(1,128)} %reshape.69), calls=%async_computation | async-start | bytes 32768 | tf_op jit(solution)/shard_map/all_to_all | solution.py:92
  124.7 2.7 copy.46
  127.4 4.8 %reshape.67 = f32[4,1,65536]{2,1,0:T(1,128)} reshape(f32[1024,8,32]{2,1,0:T(8,128)} %bitcast.117) | data formatting | bytes 2097152
  132.3 3.5 %all-to-all-start.1 = ((f32[4,1,65536]{2,1,0:T(1,128)}), f32[4,1,65536]{2,1,0:T(1,128)S(1)}, u32[]{:S(2)}, u32[]{:S(2)}) async-start(f32[4,1,65536]{2,1,0:T(1,128)} %reshape.67), calls=%async_computation.1 | async-start | bytes 2097152 | tf_op jit(solution)/shard_map/all_to_all | solution.py:116
  138.7 31.4 %all-reduce.19.cloned.1.call-done = f32[128,128]{1,0:T(8,128)} async-done(((f32[128,128]{1,0:T(8,128)}), f32[128,128]{1,0:T(8,128)}) %all-reduce.19.cloned.1.call-update) | async-done | bytes 65552 | tf_op jit(solution)/shard_map/psum | solution.py:97
  170.4 5.7 %psum.30 = f32[128]{0:T(128)S(1)} all-reduce(f32[128]{0:T(128)S(1)} %convolution_bitcast_fusion.2), channel_id=1, replica_groups=mesh['slab'=8,'mem'=4] {'mem'}, use_global_device_ids=true, to_apply=%region_4.5 | all-reduce | flops 128 | bytes 1024 | tf_op jit(solution)/shard_map/psum | solution.py:97
  176.1 21.5 %psum.31 = f32[128]{0:T(128)S(1)} all-reduce(f32[128]{0:T(128)S(1)} %psum.30), channel_id=1, replica_groups=mesh['slab'=8,'mem'=4] {'slab'}, use_global_device_ids=true, to_apply=%region_5.6 | all-reduce | flops 128 | bytes 1024 | tf_op jit(solution)/shard_map/psum | solution.py:97
  197.6 44.9 %all-reduce.21.cloned.1.call-done = f32[128,128]{1,0:T(8,128)} async-done(((f32[128,128]{1,0:T(8,128)}), f32[128,128]{1,0:T(8,128)}) %all-reduce.21.cloned.1.call-update) | async-done | bytes 65552 | tf_op jit(solution)/shard_map/psum | solution.py:97
  242.5 1.5 select_reduce_fusion
  244.0 1.7 fusion.7
  245.9 1.7 fusion.17
  253.9 3.7 %reduce.2 = f32[4,65536]{1,0:T(4,128)S(1)} reduce(f32[4,1,65536]{2,1,0:T(1,128)S(1)} %all-to-all-done.1, f32[]{:T(128)} %broadcast.130), dimensions={1}, to_apply=%all_to_all.41.reduce_sub_computation | reduce | bytes 2097156 | tf_op jit(solution)/shard_map/all_to_all | solution.py:116
  257.6 3.4 %reshape.68 = f32[1024,8,32]{2,1,0:T(8,128)} reshape(f32[4,65536]{1,0:T(4,128)S(1)} %reduce.2) | data formatting | bytes 2097152
  261.0 2.8 copy.47
  265.5 17.0 %all_to_all.52 = f32[128,8,256]{2,1,0:T(8,128)S(1)} all-to-all(f32[128,8,256]{2,1,0:T(8,128)S(1)} %copy.49), channel_id=1, replica_groups=mesh['slab'=8,'mem'=4] {'mem'}, dimensions={0} | all-to-all | bytes 2097152 | tf_op jit(solution)/shard_map/all_to_all | solution.py:119
  (100 shorter events, 25.2 us)
Async XLA Ops:
  6.5 9.8 %copy-start.2 = (f32[8]{0:T(128)S(1)}, f32[8]{0:T(128)}, u32[]{:S(2)}) copy-start(f32[8]{0:T(128)} %param.11) | copy-start | bytes 100
  6.5 10.5 %copy-start = (f32[2,8]{1,0:T(2,128)S(1)}, f32[2,8]{1,0:T(2,128)}, u32[]{:S(2)}) copy-start(f32[2,8]{1,0:T(2,128)} %param.12) | copy-start | bytes 196
  6.5 11.2 %copy-start.5 = (s32[128]{0:T(128)S(1)}, s32[128]{0:T(128)}, u32[]{:S(2)}) copy-start(s32[128]{0:T(128)} %param.13) | copy-start | bytes 1540
  6.5 11.2 %copy-start.3 = (s32[8,1024]{1,0:T(8,128)S(1)}, s32[8,1024]{1,0:T(8,128)}, u32[]{:S(2)}) copy-start(s32[8,1024]{1,0:T(8,128)} %param.10) | copy-start | bytes 98308
  6.5 26.2 %copy-start.1 = (s32[8,1024]{1,0:T(8,128)S(1)}, s32[8,1024]{1,0:T(8,128)}, u32[]{:S(2)}) copy-start(s32[8,1024]{1,0:T(8,128)} %param.9) | copy-start | bytes 98308
  9.1 23.7 %collective-permute-start = (f32[32,1,1024]{2,0,1:T(8,128)}, f32[32,1,1024]{2,0,1:T(8,128)S(1)}, u32[]{:S(2)}, u32[]{:S(2)}) collective-permute-start(f32[32,1,1024]{2,0,1:T(8,128)} %get-tuple-element.43), channel_id=1, source_target_pairs={{4,0},{8,4},{12,8},{16,12},{20,16},{24,20},{28,24},{5,1},{9,5},{13... | collective-permute-start | bytes 393224 | tf_op jit(solution)/shard_map/ppermute | solution.py:19
  10.4 22.4 %collective-permute-start.1 = (f32[32,1,1024]{2,0,1:T(8,128)}, f32[32,1,1024]{2,0,1:T(8,128)S(1)}, u32[]{:S(2)}, u32[]{:S(2)}) collective-permute-start(f32[32,1,1024]{2,0,1:T(8,128)} %get-tuple-element.42), channel_id=1, source_target_pairs={{0,4},{4,8},{8,12},{12,16},{16,20},{20,24},{24,28},{1,5},{5,9},{9,... | collective-permute-start | bytes 393224 | tf_op jit(solution)/shard_map/ppermute | solution.py:16
  33.5 7.8 %collective-permute-start.2 = (f32[32,1,1024]{2,0,1:T(8,128)S(1)}, f32[32,1,1024]{2,0,1:T(8,128)S(1)}, u32[]{:S(2)}, u32[]{:S(2)}) collective-permute-start(f32[32,1,1024]{2,0,1:T(8,128)S(1)} %get-tuple-element.39), channel_id=1, source_target_pairs={{4,0},{8,4},{12,8},{16,12},{20,16},{24,20},{28,24},{5,1},{9,5},{13... | collective-permute-start | bytes 393224 | tf_op jit(solution)/shard_map/ppermute | solution.py:19
  34.8 9.4 %collective-permute-start.3 = (f32[32,1,1024]{2,0,1:T(8,128)S(1)}, f32[32,1,1024]{2,0,1:T(8,128)S(1)}, u32[]{:S(2)}, u32[]{:S(2)}) collective-permute-start(f32[32,1,1024]{2,0,1:T(8,128)S(1)} %get-tuple-element.38), channel_id=1, source_target_pairs={{0,4},{4,8},{8,12},{12,16},{16,20},{20,24},{24,28},{1,5},{5,9},{9,... | collective-permute-start | bytes 393224 | tf_op jit(solution)/shard_map/ppermute | solution.py:16
  44.9 7.8 %collective-permute-start.4 = (f32[32,1,1024]{2,0,1:T(8,128)S(1)}, f32[32,1,1024]{2,0,1:T(8,128)S(1)}, u32[]{:S(2)}, u32[]{:S(2)}) collective-permute-start(f32[32,1,1024]{2,0,1:T(8,128)S(1)} %get-tuple-element.35), channel_id=1, source_target_pairs={{4,0},{8,4},{12,8},{16,12},{20,16},{24,20},{28,24},{5,1},{9,5},{13... | collective-permute-start | bytes 393224 | tf_op jit(solution)/shard_map/ppermute | solution.py:19
  46.2 9.5 %collective-permute-start.5 = (f32[32,1,1024]{2,0,1:T(8,128)S(1)}, f32[32,1,1024]{2,0,1:T(8,128)S(1)}, u32[]{:S(2)}, u32[]{:S(2)}) collective-permute-start(f32[32,1,1024]{2,0,1:T(8,128)S(1)} %get-tuple-element.34), channel_id=1, source_target_pairs={{0,4},{4,8},{8,12},{12,16},{16,20},{20,24},{24,28},{1,5},{5,9},{9,... | collective-permute-start | bytes 393224 | tf_op jit(solution)/shard_map/ppermute | solution.py:16
  56.4 8.1 %collective-permute-start.6 = (f32[32,1,1024]{2,0,1:T(8,128)S(1)}, f32[32,1,1024]{2,0,1:T(8,128)S(1)}, u32[]{:S(2)}, u32[]{:S(2)}) collective-permute-start(f32[32,1,1024]{2,0,1:T(8,128)S(1)} %get-tuple-element.31), channel_id=1, source_target_pairs={{4,0},{8,4},{12,8},{16,12},{20,16},{24,20},{28,24},{5,1},{9,5},{13... | collective-permute-start | bytes 393224 | tf_op jit(solution)/shard_map/ppermute | solution.py:19
  57.7 9.7 %collective-permute-start.7 = (f32[32,1,1024]{2,0,1:T(8,128)S(1)}, f32[32,1,1024]{2,0,1:T(8,128)S(1)}, u32[]{:S(2)}, u32[]{:S(2)}) collective-permute-start(f32[32,1,1024]{2,0,1:T(8,128)S(1)} %get-tuple-element.30), channel_id=1, source_target_pairs={{0,4},{4,8},{8,12},{12,16},{16,20},{20,24},{24,28},{1,5},{5,9},{9,... | collective-permute-start | bytes 393224 | tf_op jit(solution)/shard_map/ppermute | solution.py:16
  68.1 8.1 %collective-permute-start.8 = (f32[32,1,1024]{2,0,1:T(8,128)S(1)}, f32[32,1,1024]{2,0,1:T(8,128)S(1)}, u32[]{:S(2)}, u32[]{:S(2)}) collective-permute-start(f32[32,1,1024]{2,0,1:T(8,128)S(1)} %get-tuple-element.27), channel_id=1, source_target_pairs={{4,0},{8,4},{12,8},{16,12},{20,16},{24,20},{28,24},{5,1},{9,5},{13... | collective-permute-start | bytes 393224 | tf_op jit(solution)/shard_map/ppermute | solution.py:19
  69.4 9.7 %collective-permute-start.9 = (f32[32,1,1024]{2,0,1:T(8,128)S(1)}, f32[32,1,1024]{2,0,1:T(8,128)S(1)}, u32[]{:S(2)}, u32[]{:S(2)}) collective-permute-start(f32[32,1,1024]{2,0,1:T(8,128)S(1)} %get-tuple-element.26), channel_id=1, source_target_pairs={{0,4},{4,8},{8,12},{12,16},{16,20},{20,24},{24,28},{1,5},{5,9},{9,... | collective-permute-start | bytes 393224 | tf_op jit(solution)/shard_map/ppermute | solution.py:16
  79.8 8.1 %collective-permute-start.10 = (f32[32,1,1024]{2,0,1:T(8,128)S(1)}, f32[32,1,1024]{2,0,1:T(8,128)S(1)}, u32[]{:S(2)}, u32[]{:S(2)}) collective-permute-start(f32[32,1,1024]{2,0,1:T(8,128)S(1)} %get-tuple-element.23), channel_id=1, source_target_pairs={{4,0},{8,4},{12,8},{16,12},{20,16},{24,20},{28,24},{5,1},{9,5},{13... | collective-permute-start | bytes 393224 | tf_op jit(solution)/shard_map/ppermute | solution.py:19
  81.1 9.7 %collective-permute-start.11 = (f32[32,1,1024]{2,0,1:T(8,128)S(1)}, f32[32,1,1024]{2,0,1:T(8,128)S(1)}, u32[]{:S(2)}, u32[]{:S(2)}) collective-permute-start(f32[32,1,1024]{2,0,1:T(8,128)S(1)} %get-tuple-element.22), channel_id=1, source_target_pairs={{0,4},{4,8},{8,12},{12,16},{16,20},{20,24},{24,28},{1,5},{5,9},{9,... | collective-permute-start | bytes 393224 | tf_op jit(solution)/shard_map/ppermute | solution.py:16
  91.5 8.1 %collective-permute-start.12 = (f32[32,1,1024]{2,0,1:T(8,128)S(1)}, f32[32,1,1024]{2,0,1:T(8,128)S(1)}, u32[]{:S(2)}, u32[]{:S(2)}) collective-permute-start(f32[32,1,1024]{2,0,1:T(8,128)S(1)} %get-tuple-element.19), channel_id=1, source_target_pairs={{4,0},{8,4},{12,8},{16,12},{20,16},{24,20},{28,24},{5,1},{9,5},{13... | collective-permute-start | bytes 393224 | tf_op jit(solution)/shard_map/ppermute | solution.py:19
  92.8 9.7 %collective-permute-start.13 = (f32[32,1,1024]{2,0,1:T(8,128)S(1)}, f32[32,1,1024]{2,0,1:T(8,128)S(1)}, u32[]{:S(2)}, u32[]{:S(2)}) collective-permute-start(f32[32,1,1024]{2,0,1:T(8,128)S(1)} %get-tuple-element.18), channel_id=1, source_target_pairs={{0,4},{4,8},{8,12},{12,16},{16,20},{20,24},{24,28},{1,5},{5,9},{9,... | collective-permute-start | bytes 393224 | tf_op jit(solution)/shard_map/ppermute | solution.py:16
  103.3 8.1 %collective-permute-start.14 = (f32[32,1,1024]{2,0,1:T(8,128)S(1)}, f32[32,1,1024]{2,0,1:T(8,128)S(1)}, u32[]{:S(2)}, u32[]{:S(2)}) collective-permute-start(f32[32,1,1024]{2,0,1:T(8,128)S(1)} %get-tuple-element.15), channel_id=1, source_target_pairs={{4,0},{8,4},{12,8},{16,12},{20,16},{24,20},{28,24},{5,1},{9,5},{13... | collective-permute-start | bytes 393224 | tf_op jit(solution)/shard_map/ppermute | solution.py:19
  104.6 9.7 %collective-permute-start.15 = (f32[32,1,1024]{2,0,1:T(8,128)S(1)}, f32[32,1,1024]{2,0,1:T(8,128)S(1)}, u32[]{:S(2)}, u32[]{:S(2)}) collective-permute-start(f32[32,1,1024]{2,0,1:T(8,128)S(1)} %get-tuple-element.14), channel_id=1, source_target_pairs={{0,4},{4,8},{8,12},{12,16},{16,20},{20,24},{24,28},{1,5},{5,9},{9,... | collective-permute-start | bytes 393224 | tf_op jit(solution)/shard_map/ppermute | solution.py:16
  114.3 10.4 %copy-start.4 = (f32[128]{0:T(128)S(1)}, f32[128]{0:T(128)}, u32[]{:S(2)}) copy-start(f32[128]{0:T(128)} %param.15) | copy-start | bytes 1540
  121.2 11.1 %all-to-all-start = ((f32[4,1,1024]{2,1,0:T(1,128)}), f32[4,1,1024]{2,1,0:T(1,128)S(1)}, u32[]{:S(2)}, u32[]{:S(2)}) async-start(f32[4,1,1024]{2,1,0:T(1,128)} %reshape.69), calls=%async_computation | async-start | bytes 32768 | tf_op jit(solution)/shard_map/all_to_all | solution.py:92
  127.4 42.8 %copy-start.6 = (f32[128]{0:T(128)S(1)}, f32[128]{0:T(128)}, u32[]{:S(2)}) copy-start(f32[128]{0:T(128)} %param.14) | copy-start | bytes 1540
  132.3 121.6 %all-to-all-start.1 = ((f32[4,1,65536]{2,1,0:T(1,128)}), f32[4,1,65536]{2,1,0:T(1,128)S(1)}, u32[]{:S(2)}, u32[]{:S(2)}) async-start(f32[4,1,65536]{2,1,0:T(1,128)} %reshape.67), calls=%async_computation.1 | async-start | bytes 2097152 | tf_op jit(solution)/shard_map/all_to_all | solution.py:116
  135.8 34.3 %all-reduce.19.cloned.1.call-start = ((), (), s32[]{:S(2)}) async-start(), calls=%async_computation.3 | async-start | bytes 131072 | tf_op jit(solution)/shard_map/psum | solution.py:97
  138.5 104.0 %all-reduce.21.cloned.1.call-start = ((), (), s32[]{:S(2)}) async-start(), calls=%async_computation.4 | async-start | bytes 131072 | tf_op jit(solution)/shard_map/psum | solution.py:97
Sparse Core Ops, SparseCore 0:
  139.0 31.1 all-reduce.18
  173.9 68.4 all-reduce.20
